TPU v7x, 32 devices: a whole 2x2x4 slice. The times are simulated.
32 devices in a mesh: groups: 2 (over x), lon: 16 (over z, y, core).
Axes of the slice: x: 2, y: 2, z: 4, core: 2. Of those that a mesh axis runs over, the one named last changes fastest.
Arguments:
- white_noise: float32 [32, 256, 1024], P('groups', 'lon'), parts along dimension 0, may hold values from -6 to 6
- kappa_sq: float32 [256, 1024], P('lon'), may hold values from 0.05 to 1
- station_lat: float32 [16384], P(('groups', 'lon')), parts along dimension 0, may hold values from 0 to 1024
- station_lon: float32 [16384], P(('groups', 'lon')), parts along dimension 0, may hold values from 0 to 16
- station_weights: float32 [32, 8192], P('groups', 'lon'), parts along dimension 0, may hold values from -6 to 6
- station_count: int32 [32], P(('groups', 'lon')), parts along dimension 0, may hold values from 32 to 512, as said below
Outputs:
- posterior: float32 [32, 256, 1024], P('groups', 'lon'), parts along dimension 0
There are 2 independent parts, one for each index of `groups`. A program takes and returns all parts, laid end to end along the dimension named above; an argument that names none is the same for every part. Nothing has to cross between parts.
Inputs may be any that keep to these rules, and one draw needn't show every extreme that they name: `station_count`: each tile's live stations fill its first slots; at least one tile has all 512 slots live.
All inputs are finite; a program needn't handle non-finite values.
Results may differ from a plain program's by a relative error of at most 0.0003.
Values sent between devices are 32-bit elements; how exact they have to be, the bound alone decides.
No kernel may reach another device: no remote copies, remote signals or barrier semaphores. Data moves between devices by JAX's collectives and lax.ppermute only.
A program may use at most 64 MiB of HBM per device.

v0:
```python
import math

import jax
import jax.numpy as jnp
import numpy as np
from jax import lax
from jax.experimental import pallas as pl
from jax.experimental.pallas import tpu as pltpu
from jax.sharding import PartitionSpec as P

PASSES = 8
HOPS = 2
CHEB = (0.62, -0.41, 0.3, -0.22, 0.16, -0.115, 0.08, -0.055, 0.04)
LOG2E = math.log2(math.e)
FAR = 4096.0
CH = 32
UNROLL = 24
LANES = 128
BLOCK = 128
ROOM = 24 * 2**20
PAD = 8
WIDE = 8


def horner_coeffs():
    powers = np.polynomial.chebyshev.cheb2poly(np.array(CHEB))
    lead = powers[PASSES]
    inner = [float(powers[k] / lead * (-4.5) ** (PASSES - k)) for k in range(PASSES)]
    return inner, float(lead / 4.5**PASSES)


def split3(value):
    high = value.astype(jnp.bfloat16)
    rest = value - high.astype(jnp.float32)
    middle = rest.astype(jnp.bfloat16)
    low = (rest - middle.astype(jnp.float32)).astype(jnp.bfloat16)
    return high, middle, low


def station_kernel(
    p0, p1, p2, p3, p4, out_ref,
    table_v, table_s, data, sorted_s, merged, wts, latb, dlon2, stage, starts, sem_s,
    *, samples, width, height, slots,
):
    packs = (p0, p1, p2, p3, p4)
    lists = len(packs)
    radius = float(HOPS * width)
    band = int(radius)
    bands = height // band
    rows_m = (bands + 1 + 7) // 8 * 8
    scale = LOG2E / radius
    groups = band * width // LANES
    per_group = LANES // band
    index_m = lax.broadcasted_iota(jnp.int32, (rows_m, slots), 0).astype(jnp.float32)
    equal, below, onehot = [], [], []
    for pack in packs:
        lat = pack[samples : samples + 1, :]
        bucket = jnp.minimum(jnp.floor(lat * (1.0 / radius)), float(bands - 1))
        bucket = jnp.where(lat > FAR * 0.5, float(bands), bucket)
        bucket = jnp.broadcast_to(bucket, (rows_m, slots))
        equal.append(jnp.where(bucket == index_m, 1.0, 0.0))
        below.append(jnp.where(bucket < index_m, 1.0, 0.0).astype(jnp.bfloat16))
    before = lax.broadcasted_iota(jnp.int32, (slots, slots), 0) < lax.broadcasted_iota(
        jnp.int32, (slots, slots), 1
    )
    before = jnp.where(before, 1.0, 0.0).astype(jnp.bfloat16)
    all_below = jnp.concatenate(below, axis=0)
    inside = jnp.dot(
        jnp.concatenate(equal, axis=0).astype(jnp.bfloat16), before, preferred_element_type=jnp.float32
    )
    base = jnp.dot(all_below, jnp.ones((slots, LANES), jnp.bfloat16), preferred_element_type=jnp.float32)
    counts = lax.dot_general(
        jnp.ones((8, slots), jnp.bfloat16), all_below, (((1,), (1,)), ((), ())),
        preferred_element_type=jnp.float32,
    )
    table_v[...] = counts.astype(jnp.int32)
    copy = pltpu.make_async_copy(table_v, table_s, sem_s)
    copy.start()
    ranks = []
    for index in range(lists):
        rows = slice(index * rows_m, (index + 1) * rows_m)
        start = base[rows]
        start = jnp.concatenate([start] * (slots // LANES), axis=1)
        ranks.append(jnp.sum(equal[index] * (inside[rows] + start), axis=0, keepdims=True))

    factor = 4.0 * math.exp(-1.0) / LOG2E**5
    for index, pack in enumerate(packs):
        weights = pack[0:samples, :] * factor
        w_high = weights.astype(jnp.bfloat16)
        w_low = (weights - w_high.astype(jnp.float32)).astype(jnp.bfloat16)
        lat = pack[samples : samples + 1, :]
        lon = pack[samples + 1 : samples + 2, :] + float((index - HOPS) * width)
        parts = split3(lat) + split3(lon)
        parts = [part.astype(jnp.float32) for part in parts]
        filler = jnp.zeros((LANES - 2 * samples - 6, slots), jnp.float32)
        block = jnp.concatenate(
            [w_high.astype(jnp.float32), w_low.astype(jnp.float32)] + parts + [filler], axis=0
        )
        data[index] = block.astype(jnp.bfloat16)

    for m in range(bands + 1):
        stage[m] = jnp.zeros((samples, groups * LANES), jnp.float32)
    copy.wait()

    row_p = lax.broadcasted_iota(jnp.int32, (LANES, slots), 0).astype(jnp.float32)
    longest = table_s[0, bands]
    for index in range(1, lists):
        longest = jnp.maximum(longest, table_s[0, index * rows_m + bands])

    def sort_block(block, carry):
        first = block * LANES
        for index in range(lists):
            pick = ranks[index] - first.astype(jnp.float32)
            pick = jnp.where(jnp.broadcast_to(pick, (LANES, slots)) == row_p, 1.0, 0.0)
            moved = lax.dot_general(
                pick.astype(jnp.bfloat16), data[index], (((1,), (1,)), ((), ())),
                preferred_element_type=jnp.float32,
            )
            sorted_s[pl.ds(pl.multiple_of(index * slots + first, LANES), LANES), :] = moved
        return carry

    def sort_pair(pair, carry):
        return sort_block(2 * pair + 1, sort_block(2 * pair, carry))

    lax.fori_loop(0, (longest + 2 * LANES - 1) // (2 * LANES), sort_pair, 0)

    step = 32

    def merge_band(m, position):
        starts[m] = position
        begins, sizes, places = [], [], []
        for index in range(lists):
            begin = table_s[0, index * rows_m + m]
            sizes.append(table_s[0, index * rows_m + m + 1] - begin)
            begins.append(index * slots + begin)
            places.append(position)
            position = position + sizes[-1]
        for index in range(lists):
            merged[pl.ds(places[index], step), :] = sorted_s[pl.ds(begins[index], step), :]
        largest = sizes[0]
        for size in sizes[1:]:
            largest = jnp.maximum(largest, size)

        @pl.when(largest > step)
        def _():
            for index in range(lists):

                def more(k, carry, index=index):
                    rows = sorted_s[pl.ds(begins[index] + k * step, step), :]
                    merged[pl.ds(places[index] + k * step, step), :] = rows
                    return carry

                lax.fori_loop(0, (sizes[index] + step - 1) // step, more, 0)

        return position

    def merge_pair(pair, position):
        return merge_band(2 * pair + 1, merge_band(2 * pair, position))

    total = lax.fori_loop(0, bands // 2, merge_pair, jnp.int32(0))
    starts[bands] = total
    lane = lax.broadcasted_iota(jnp.int32, (BLOCK, LANES), 1)
    merged[pl.ds(total, BLOCK), :] = jnp.where(lane == 2 * samples, FAR, 0.0)

    lane_row = lax.broadcasted_iota(jnp.int32, (1, LANES), 1)
    cell_in = (lane_row % band).astype(jnp.float32)
    cell_lon = (lane_row // band).astype(jnp.float32)

    row_of = lax.broadcasted_iota(jnp.int32, (LANES, 2 * LANES), 0) - 2 * samples
    part_of = lax.broadcasted_iota(jnp.int32, (LANES, 2 * LANES), 1) // LANES * 3
    gather = jnp.where((row_of >= part_of) & (row_of < part_of + 3), 1.0, 0.0).astype(jnp.bfloat16)
    turn_rows = lax.broadcasted_iota(jnp.int32, (samples, LANES), 0)
    turn_lanes = lax.broadcasted_iota(jnp.int32, (samples, LANES), 1)
    select = (turn_lanes == turn_rows) | (turn_lanes == turn_rows + samples)
    select = jnp.where(select, 1.0, 0.0).astype(jnp.bfloat16)
    is_high = lax.broadcasted_iota(jnp.int32, (CH, LANES), 1) < samples

    def prepare_pair(pair, carry):
        for half in range(2):
            prepare(2 * pair + half)
        return carry

    def prepare(block):
        first = pl.multiple_of(block * BLOCK, BLOCK)
        rows = merged[pl.ds(first, BLOCK), :]
        places = jnp.dot(rows.astype(jnp.bfloat16), gather, preferred_element_type=jnp.float32)
        latb[pl.ds(first, BLOCK), :] = places[:, 0:LANES]
        lon = places[:, LANES : 2 * LANES]
        for group in range(groups):
            offset = (lon - (cell_lon + float(group * per_group))) * scale
            dlon2[pl.ds(first, BLOCK), group * LANES : (group + 1) * LANES] = offset * offset + 1e-30
        for k in range(BLOCK // CH):
            some = rows[k * CH : (k + 1) * CH, :]
            high_rows = jnp.where(is_high, some, 0.0)
            low_rows = jnp.where(is_high, 0.0, some)
            thrice = jnp.concatenate([high_rows, high_rows, low_rows], axis=0).astype(jnp.bfloat16)
            turned = lax.dot_general(
                select, thrice, (((1,), (1,)), ((), ())), preferred_element_type=jnp.float32
            )
            wts[block * (BLOCK // CH) + k] = turned.astype(jnp.bfloat16)

    lax.fori_loop(0, total // (2 * BLOCK) + 1, prepare_pair, 0)

    def low_of(m):
        return starts[jnp.maximum(m - 1, 0)] // CH

    def high_of(m):
        return jnp.maximum((starts[jnp.minimum(m + 2, bands)] + CH - 1) // CH, low_of(m) + 1)

    def eval_items(carry):
        m, chunk = carry
        for _ in range(UNROLL):
            first = pl.multiple_of(chunk * CH, CH)
            offset = (latb[pl.ds(first, CH), :] - (cell_in + (m * band).astype(jnp.float32))) * scale
            offset = offset * offset
            kerns = []
            for group in range(groups):
                square = offset + dlon2[pl.ds(first, CH), group * LANES : (group + 1) * LANES]
                taper = jnp.maximum(LOG2E - square * lax.rsqrt(square), 0.0)
                twice = taper * taper
                kerns.append((twice * twice) * (1.25 * LOG2E - taper) * jnp.exp2(taper))
            kern = jnp.concatenate(kerns, axis=1)
            high_part = kern.astype(jnp.bfloat16)
            low_part = (kern - high_part.astype(jnp.float32)).astype(jnp.bfloat16)
            parts = jnp.concatenate([high_part, low_part, high_part], axis=0)
            stage[m] += jnp.dot(wts[chunk], parts, preferred_element_type=jnp.float32)
            done = chunk + 1 >= high_of(m)
            after = jnp.minimum(m + 1, bands)
            chunk = jnp.where(done, low_of(after), chunk + 1)
            chunk = jnp.where(after == bands, jnp.where(done, 0, chunk), chunk)
            m = jnp.where(done, after, m)
        return m, chunk

    first_item = (jnp.int32(0), low_of(jnp.int32(0)))
    lax.while_loop(lambda carry: carry[0] < bands, eval_items, first_item)

    part = lax.broadcasted_iota(jnp.int32, (samples, LANES), 1) // band

    def lay_out_pair(pair, carry):
        for half in range(2):
            lay_out(2 * pair + half)
        return carry

    def lay_out(block):
        at = pl.multiple_of(block * LANES, LANES)
        for group in range(groups):
            pieces = [
                stage[block * per_group + j, :, group * LANES : (group + 1) * LANES]
                for j in range(per_group)
            ]
            bit = 1
            while bit < per_group:
                keep = (part & bit) == 0
                for j in range(per_group):
                    if j & bit == 0:
                        first, second = pieces[j], pieces[j | bit]
                        pieces[j] = jnp.where(keep, first, pltpu.roll(second, bit * band, 1))
                        pieces[j | bit] = jnp.where(keep, pltpu.roll(first, LANES - bit * band, 1), second)
                bit *= 2
            for j in range(per_group):
                out_ref[group * per_group + j, :, pl.ds(at, LANES)] = pieces[j]

    lax.fori_loop(0, height // (2 * LANES), lay_out_pair, 0)


def pack_kernel(lat_hbm, lon_hbm, weights_hbm, count_ref, pack_ref, lat, sems, *, samples, slots):
    copies = [
        pltpu.make_async_copy(lat_hbm, lat, sems.at[0]),
        pltpu.make_async_copy(lon_hbm, pack_ref.at[samples + 1 : samples + 2], sems.at[1]),
        pltpu.make_async_copy(weights_hbm, pack_ref.at[0:samples], sems.at[2]),
    ]
    for copy in copies:
        copy.start()
    for copy in copies:
        copy.wait()
    slot = lax.broadcasted_iota(jnp.int32, (1, slots), 1)
    pack_ref[samples : samples + 1, :] = jnp.where(slot < count_ref[0], lat[...], FAR)


def turn_kernel(
    x_hbm, kappa_hbm, low_ref, high_ref, beta_ref, noise, kap, sem_x, sem_k, *, samples, width, height
):
    segments = height // LANES
    tall = height * samples // LANES
    copies = [pltpu.make_async_copy(x_hbm.at[:, c, :], noise.at[c], sem_x.at[c]) for c in range(width)]
    copies.append(pltpu.make_async_copy(kappa_hbm, kap, sem_k))
    for copy in copies:
        copy.start()
    copies[-1].wait()
    for column in range(width):
        half = (low_ref, high_ref)[column // PASSES]
        for i in range(segments):
            piece = kap[column : column + 1, i * LANES : (i + 1) * LANES]
            half[column % PASSES, tall + i : tall + i + 1, :] = piece
        beta_ref[column] = spread_kappa(half.at[column % PASSES], tall, samples, segments)
    for column in range(width):
        copies[column].wait()
    for column in range(width):
        half = (low_ref, high_ref)[column // PASSES]
        pieces = [noise[column, :, i * LANES : (i + 1) * LANES] for i in range(segments)]
        half[column % PASSES, 0:tall, :] = jnp.concatenate(pieces, axis=0).T


def spread_kappa(ref, start, samples, segments):
    rows = [ref[start + i : start + i + 1, :] - 0.5 for i in range(segments)]
    rows = [jnp.broadcast_to(row, (samples, LANES)) for row in rows]
    return jnp.concatenate(rows, axis=0).T


def prior_kernel(
    left_ref, low_ref, high_ref, right_ref, beta_ref, upd, out_hbm,
    noise, betas, first_y, second_y, result, sem_out, *, samples, width, height,
):
    halo = PASSES
    inner, outer = horner_coeffs()
    segments = height // LANES
    tall = height * samples // LANES
    columns = width + 2 * halo
    pitch = tall + 2 * PAD
    lane = lax.broadcasted_iota(jnp.int32, (8, LANES), 1)
    sub = lax.broadcasted_iota(jnp.int32, (8, LANES), 0)
    on_top, on_bottom = sub == 0, sub == 7
    inner_low = lane >= samples
    inner_high = lane < LANES - samples

    def at(base, offset):
        return pl.ds(pl.multiple_of(base + offset, 8), 8)

    def bring(column, carry):
        for k, ref in enumerate((left_ref, low_ref, high_ref, right_ref)):
            base = (k * halo + column) * pitch
            noise[pl.ds(pl.multiple_of(base + PAD, 8), tall), :] = ref[column, 0:tall, :]
        betas[column] = spread_kappa(left_ref.at[column], tall, samples, segments)
        betas[column + halo] = beta_ref[column]
        betas[column + 2 * halo] = beta_ref[column + halo]
        betas[column + 3 * halo] = spread_kappa(right_ref.at[column], tall, samples, segments)
        return carry

    def bring_pair(pair, carry):
        return bring(2 * pair + 1, bring(2 * pair, carry))

    lax.fori_loop(0, halo // 2, bring_pair, 0)
    source = noise
    for turn in range(PASSES):
        target = (first_y, second_y)[turn % 2]
        level = PASSES - 1 - turn
        last = turn == PASSES - 1

        def sweep(column, count, source=source, target=target, level=level, last=last):
            base = column * pitch
            saved = [[] for _ in range(count)]
            for r in range(tall // 8):
                row = PAD + r * 8
                line = [source[at(base, t * pitch + row), :] for t in range(-1, count + 1)]
                for t in range(count):
                    north = source[pl.ds(base + (t * pitch + row - 1), 8), :]
                    south = source[pl.ds(base + (t * pitch + row + 1), 8), :]
                    if r == 0:
                        end = source[pl.ds(base + (t * pitch + PAD + tall - 1), 8), :]
                        end = jnp.where(inner_low, pltpu.roll(end, samples, 1), 0.0)
                        north = jnp.where(on_top, end, north)
                    if r == tall // 8 - 1:
                        end = source[pl.ds(base + (t * pitch + PAD - 7), 8), :]
                        end = jnp.where(inner_high, pltpu.roll(end, LANES - samples, 1), 0.0)
                        south = jnp.where(on_bottom, end, south)
                    beside = (north + south) + (line[t] + line[t + 2])
                    value = beside - betas[column + t, r * 8 : r * 8 + 8, :] * line[t + 1]
                    value = value + inner[level] * noise[at(base, t * pitch + row), :]
                    if last:
                        saved[t].append(value)
                    else:
                        target[at(base, t * pitch + row), :] = value
            for t in range(count if last else 0):
                own = column + t - halo
                turned = jnp.concatenate(saved[t], axis=0).T
                for i in range(segments):
                    lanes = slice(i * LANES, (i + 1) * LANES)
                    value = outer * turned[i * samples : (i + 1) * samples, :] + upd[own, :, lanes]
                    result[own, :, lanes] = value
                pltpu.make_async_copy(result.at[own], out_hbm.at[:, own, :], sem_out.at[own]).start()

        def step_wide(step, carry, sweep=sweep, turn=turn):
            sweep(turn + 1 + WIDE * step, WIDE)
            return carry

        count = columns - 2 * (turn + 1)
        lax.fori_loop(0, count // WIDE, step_wide, 0)
        if count % WIDE:
            sweep(jnp.int32(turn + 1 + count - count % WIDE), count % WIDE)
        source = target
    for column in range(width):
        pltpu.make_async_copy(result.at[column], out_hbm.at[:, column, :], sem_out.at[column]).wait()


def shift_to(value, axis, steps):
    count = lax.axis_size(axis)
    return lax.ppermute(value, axis, [(source, (source + steps) % count) for source in range(count)])


def local(white_noise, kappa_sq, station_lat, station_lon, station_weights, station_count):
    samples, width, height = white_noise.shape
    slots = station_lat.shape[0]
    halo = PASSES
    anywhere = pl.BlockSpec(memory_space=pl.ANY)
    whole = pl.BlockSpec(memory_space=pltpu.VMEM)
    hbm = pl.BlockSpec(memory_space=pltpu.HBM)

    def in_hbm(items):
        return [pltpu.with_memory_space_constraint(item, pltpu.HBM) for item in items]

    pack = pl.pallas_call(
        lambda *refs: pack_kernel(*refs, samples=samples, slots=slots),
        out_shape=pltpu.VMEM((samples + 2, slots), jnp.float32),
        in_specs=[hbm] * 3 + [pl.BlockSpec(memory_space=pltpu.SMEM)],
        out_specs=whole,
        scratch_shapes=[pltpu.VMEM((1, slots), jnp.float32), pltpu.SemaphoreType.DMA((3,))],
        compiler_params=pltpu.CompilerParams(vmem_limit_bytes=ROOM),
        name="pack",
    )(*in_hbm((station_lat[None], station_lon[None], station_weights)), station_count)
    later = lax.optimization_barrier((pack, white_noise, kappa_sq))
    pack = later[0]
    packs = []
    for step in range(-HOPS, HOPS + 1):
        packs.append(pack if step == 0 else shift_to(pack, "lon", -step))

    segments = height // LANES
    tall = height * samples // LANES
    half = pltpu.VMEM((halo, tall + segments, LANES), jnp.float32)
    low, high, beta = pl.pallas_call(
        lambda *refs: turn_kernel(*refs, samples=samples, width=width, height=height),
        out_shape=(half, half, pltpu.VMEM((width, tall, LANES), jnp.float32)),
        in_specs=[hbm] * 2,
        out_specs=(whole, whole, whole),
        scratch_shapes=[
            pltpu.VMEM((width, samples, height), jnp.float32),
            pltpu.VMEM((width, height), jnp.float32),
            pltpu.SemaphoreType.DMA((width,)),
            pltpu.SemaphoreType.DMA,
        ],
        compiler_params=pltpu.CompilerParams(vmem_limit_bytes=ROOM),
        name="turn",
    )(*in_hbm(later[1:]))
    left = shift_to(high, "lon", 1)
    right = shift_to(low, "lon", -1)
    packs = [pltpu.with_memory_space_constraint(item, pltpu.VMEM) for item in packs]

    lists = 2 * HOPS + 1
    band = HOPS * width
    bands = height // band
    rows_m = (bands + 1 + 7) // 8 * 8
    room = lists * slots + 2 * LANES
    upd = pl.pallas_call(
        lambda *refs: station_kernel(*refs, samples=samples, width=width, height=height, slots=slots),
        out_shape=pltpu.VMEM((width, samples, height), jnp.float32),
        in_specs=[whole] * lists,
        out_specs=whole,
        scratch_shapes=[
            pltpu.VMEM((8, lists * rows_m), jnp.int32),
            pltpu.SMEM((8, lists * rows_m), jnp.int32),
            pltpu.VMEM((lists, LANES, slots), jnp.bfloat16),
            pltpu.VMEM((room, LANES), jnp.float32),
            pltpu.VMEM((room, LANES), jnp.float32),
            pltpu.VMEM((room // CH, samples, 3 * CH), jnp.bfloat16),
            pltpu.VMEM((room, LANES), jnp.float32),
            pltpu.VMEM((room, band * width), jnp.float32),
            pltpu.VMEM((bands + 1, samples, band * width), jnp.float32),
            pltpu.SMEM((bands + 1,), jnp.int32),
            pltpu.SemaphoreType.DMA,
        ],
        compiler_params=pltpu.CompilerParams(vmem_limit_bytes=ROOM),
        cost_estimate=pl.CostEstimate(flops=10000000000, transcendentals=10**7, bytes_accessed=2 * 10**6),
        name="stations",
    )(*packs)
    columns = width + 2 * halo
    field = pltpu.VMEM(((columns + 2) * (tall + 2 * PAD), LANES), jnp.float32)
    fields = [left, low, high, right, beta, upd]
    fields = [pltpu.with_memory_space_constraint(item, pltpu.VMEM) for item in fields]
    return pl.pallas_call(
        lambda *refs: prior_kernel(*refs, samples=samples, width=width, height=height),
        out_shape=jax.ShapeDtypeStruct((samples, width, height), jnp.float32),
        in_specs=[whole] * 6,
        out_specs=anywhere,
        scratch_shapes=[
            field,
            pltpu.VMEM((columns + 2, tall, LANES), jnp.float32),
            field,
            field,
            pltpu.VMEM((width, samples, height), jnp.float32),
            pltpu.SemaphoreType.DMA((width,)),
        ],
        compiler_params=pltpu.CompilerParams(vmem_limit_bytes=ROOM),
        name="prior",
    )(*fields)


def solution(mesh):
    in_specs = (
        P("groups", "lon", None),
        P("lon", None),
        P(("groups", "lon")),
        P(("groups", "lon")),
        P("groups", "lon"),
        P(("groups", "lon")),
    )
    out_specs = P("groups", "lon", None)
    return jax.shard_map(local, mesh=mesh, in_specs=in_specs, out_specs=out_specs, check_vma=False)
```

profile of v0, /device:TPU:1, one launch (start us, length us, event | category | flops | bytes accessed | tf_op | source)
XLA Modules:
  0.0 31.7 jit_solution(10125165522407526318)
XLA Ops:
  0.7 0.8 %pack.1.refs_2_ = f32[18,512]{1,0:T(8,128)S(1)} custom-call(f32[1,512]{1,0:T(1,128)} %bitcast.2, f32[1,512]{1,0:T(1,128)} %bitcast.3, f32[16,512]{1,0:T(8,128)} %refs_2_.1, s32[1]{0:T(128)S(6)} %copy.7.refs_3_), custom_call_target="tpu_custom_call" | custom-call | tf_op jit(solution)/shard_map/pack/pallas_call | solution.py:411
  1.5 5.2 %collective-permute-start.5 = (f32[18,512]{1,0:T(8,128)S(1)}, f32[18,512]{1,0:T(8,128)S(1)}, u32[]{:S(2)}, u32[]{:S(2)}) collective-permute-start(f32[18,512]{1,0:T(8,128)S(1)} %pack.1.refs_2_), channel_id=1, source_target_pairs={{0,14},{1,15},{2,0},{3,1},{4,2},{5,3},{6,4},{7,5},{8,6},{9,7},{10,... | collective-permute-start | bytes 110600 | tf_op jit(solution)/shard_map/ppermute | solution.py:397
  6.6 1.0 %collective-permute-start.4 = (f32[18,512]{1,0:T(8,128)S(1)}, f32[18,512]{1,0:T(8,128)S(1)}, u32[]{:S(2)}, u32[]{:S(2)}) collective-permute-start(f32[18,512]{1,0:T(8,128)S(1)} %pack.1.refs_2_), channel_id=1, source_target_pairs={{0,15},{1,0},{2,1},{3,2},{4,3},{5,4},{6,5},{7,6},{8,7},{9,8},{10,9... | collective-permute-start | bytes 110600 | tf_op jit(solution)/shard_map/ppermute | solution.py:397
  7.6 0.8 %collective-permute-start.3 = (f32[18,512]{1,0:T(8,128)S(1)}, f32[18,512]{1,0:T(8,128)S(1)}, u32[]{:S(2)}, u32[]{:S(2)}) collective-permute-start(f32[18,512]{1,0:T(8,128)S(1)} %pack.1.refs_2_), channel_id=1, source_target_pairs={{0,1},{1,2},{2,3},{3,4},{4,5},{5,6},{6,7},{7,8},{8,9},{9,10},{10,1... | collective-permute-start | bytes 110600 | tf_op jit(solution)/shard_map/ppermute | solution.py:397
  8.4 0.0 collective-permute-start.2
  8.4 2.2 %turn.1 = (f32[8,136,128]{2,1,0:T(8,128)S(1)}, f32[8,136,128]{2,1,0:T(8,128)S(1)}, f32[16,128,128]{2,1,0:T(8,128)S(1)}) custom-call(f32[16,16,1024]{2,1,0:T(8,128)} %refs_0_, f32[16,1024]{1,0:T(8,128)} %refs_1_), custom_call_target="tpu_custom_call" | custom-call | tf_op jit(solution)/shard_map/turn/pallas_call | solution.py:429
  10.6 0.1 collective-permute-start
  10.7 0.0 collective-permute-done.5.refs_4_
  10.7 0.5 %collective-permute-start.1 = (f32[8,136,128]{2,1,0:T(8,128)S(1)}, f32[8,136,128]{2,1,0:T(8,128)S(1)}, u32[]{:S(2)}, u32[]{:S(2)}) collective-permute-start(f32[8,136,128]{2,1,0:T(8,128)S(1)} %get-tuple-element.14.refs_1_), channel_id=1, source_target_pairs={{0,15},{1,0},{2,1},{3,2},{4,3},{5,4},{6,5},{7,6},{8,7},{9,8},{10,9... | collective-permute-start | bytes 1671176 | tf_op jit(solution)/shard_map/ppermute | solution.py:397
  11.2 0.0 collective-permute-done.4.refs_3_
  11.2 0.0 collective-permute-done.3.refs_1_
  11.2 3.4 %collective-permute-done.2.refs_0_ = f32[18,512]{1,0:T(8,128)S(1)} collective-permute-done((f32[18,512]{1,0:T(8,128)S(1)}, f32[18,512]{1,0:T(8,128)S(1)}, u32[]{:S(2)}, u32[]{:S(2)}) %collective-permute-start.2) | collective-permute-done | bytes 36896 | tf_op jit(solution)/shard_map/ppermute | solution.py:397
  14.7 8.5 %stations.1.refs_5_ = f32[16,16,1024]{2,1,0:T(8,128)S(1)} custom-call(f32[18,512]{1,0:T(8,128)S(1)} %collective-permute-done.2.refs_0_, f32[18,512]{1,0:T(8,128)S(1)} %collective-permute-done.3.refs_1_, f32[18,512]{1,0:T(8,128)S(1)} %pack.1.refs_2_, f32[18,512]{1,0:T(8,128)S(1)} %collective-permute-done.4.refs_3_, f32[18,512]{1,0:T(8,128)S(1)} %collective-permute-done.5.refs_4_), custom_call_target="tpu_custom_call" | custom-call | flops 10000000000 | bytes 2000000 | tf_op jit(solution)/shard_map/stations/pallas_call | solution.py:452
  23.2 0.0 collective-permute-done.refs_0_
  23.2 3.3 %collective-permute-done.1.refs_3_ = f32[8,136,128]{2,1,0:T(8,128)S(1)} collective-permute-done((f32[8,136,128]{2,1,0:T(8,128)S(1)}, f32[8,136,128]{2,1,0:T(8,128)S(1)}, u32[]{:S(2)}, u32[]{:S(2)}) %collective-permute-start.1) | collective-permute-done | bytes 557088 | tf_op jit(solution)/shard_map/ppermute | solution.py:397
  26.5 5.2 %prior.1 = f32[16,16,1024]{2,1,0:T(8,128)} custom-call(f32[8,136,128]{2,1,0:T(8,128)S(1)} %collective-permute-done.refs_0_, f32[8,136,128]{2,1,0:T(8,128)S(1)} %get-tuple-element.14.refs_1_, f32[8,136,128]{2,1,0:T(8,128)S(1)} %get-tuple-element.13.refs_2_, f32[8,136,128]{2,1,0:T(8,128)S(1)} %collective-permute-done.1.refs_3_, ...), custom_call_target="tpu_custom_call" | custom-call | tf_op jit(solution)/shard_map/prior/pallas_call | solution.py:478
Async XLA Ops:
  1.5 9.2 %collective-permute-start.5 = (f32[18,512]{1,0:T(8,128)S(1)}, f32[18,512]{1,0:T(8,128)S(1)}, u32[]{:S(2)}, u32[]{:S(2)}) collective-permute-start(f32[18,512]{1,0:T(8,128)S(1)} %pack.1.refs_2_), channel_id=1, source_target_pairs={{0,14},{1,15},{2,0},{3,1},{4,2},{5,3},{6,4},{7,5},{8,6},{9,7},{10,... | collective-permute-start | bytes 110600 | tf_op jit(solution)/shard_map/ppermute | solution.py:397
  6.6 4.6 %collective-permute-start.4 = (f32[18,512]{1,0:T(8,128)S(1)}, f32[18,512]{1,0:T(8,128)S(1)}, u32[]{:S(2)}, u32[]{:S(2)}) collective-permute-start(f32[18,512]{1,0:T(8,128)S(1)} %pack.1.refs_2_), channel_id=1, source_target_pairs={{0,15},{1,0},{2,1},{3,2},{4,3},{5,4},{6,5},{7,6},{8,7},{9,8},{10,9... | collective-permute-start | bytes 110600 | tf_op jit(solution)/shard_map/ppermute | solution.py:397
  7.6 3.6 %collective-permute-start.3 = (f32[18,512]{1,0:T(8,128)S(1)}, f32[18,512]{1,0:T(8,128)S(1)}, u32[]{:S(2)}, u32[]{:S(2)}) collective-permute-start(f32[18,512]{1,0:T(8,128)S(1)} %pack.1.refs_2_), channel_id=1, source_target_pairs={{0,1},{1,2},{2,3},{3,4},{4,5},{5,6},{6,7},{7,8},{8,9},{9,10},{10,1... | collective-permute-start | bytes 110600 | tf_op jit(solution)/shard_map/ppermute | solution.py:397
  8.4 6.3 %collective-permute-start.2 = (f32[18,512]{1,0:T(8,128)S(1)}, f32[18,512]{1,0:T(8,128)S(1)}, u32[]{:S(2)}, u32[]{:S(2)}) collective-permute-start(f32[18,512]{1,0:T(8,128)S(1)} %pack.1.refs_2_), channel_id=1, source_target_pairs={{0,2},{1,3},{2,4},{3,5},{4,6},{5,7},{6,8},{7,9},{8,10},{9,11},{10,... | collective-permute-start | bytes 110600 | tf_op jit(solution)/shard_map/ppermute | solution.py:397
  10.6 12.5 %collective-permute-start = (f32[8,136,128]{2,1,0:T(8,128)S(1)}, f32[8,136,128]{2,1,0:T(8,128)S(1)}, u32[]{:S(2)}, u32[]{:S(2)}) collective-permute-start(f32[8,136,128]{2,1,0:T(8,128)S(1)} %get-tuple-element.13.refs_2_), channel_id=1, source_target_pairs={{0,1},{1,2},{2,3},{3,4},{4,5},{5,6},{6,7},{7,8},{8,9},{9,10},{10,1... | collective-permute-start | bytes 1671176 | tf_op jit(solution)/shard_map/ppermute | solution.py:397
  10.7 15.8 %collective-permute-start.1 = (f32[8,136,128]{2,1,0:T(8,128)S(1)}, f32[8,136,128]{2,1,0:T(8,128)S(1)}, u32[]{:S(2)}, u32[]{:S(2)}) collective-permute-start(f32[8,136,128]{2,1,0:T(8,128)S(1)} %get-tuple-element.14.refs_1_), channel_id=1, source_target_pairs={{0,15},{1,0},{2,1},{3,2},{4,3},{5,4},{6,5},{7,6},{8,7},{9,8},{10,9... | collective-permute-start | bytes 1671176 | tf_op jit(solution)/shard_map/ppermute | solution.py:397
where the time goes:
time: 32 us; the launch traced here: 31.7 us
  Pallas kernels  16.7 us (52%)
  starting transfers between devices  7.46 us (23%)
  waiting for transfers between devices  6.79 us (21%)
  between operations  0.7 us (2%)
    pallas_call x1, Pallas kernels, local(): pl.pallas_call(lambda *refs: station_kernel(*refs, samples=samples, width...  8.48 us
    ppermute x6, starting transfers between devices, shift_to(): lax.ppermute(value, axis, [(source, (source + steps) % count) for source...  7.46 us
    ppermute x6, waiting for transfers between devices, shift_to(): lax.ppermute(value, axis, [(source, (source + steps) % count) for source...  6.79 us
    pallas_call x1, Pallas kernels, local(): pl.pallas_call(lambda *refs: prior_kernel(*refs, samples=samples, width=w...  5.17 us
    pallas_call x1, Pallas kernels, local(): pl.pallas_call(lambda *refs: turn_kernel(*refs, samples=samples, width=wi...  2.24 us
    pallas_call x1, Pallas kernels, local(): pl.pallas_call(lambda *refs: pack_kernel(*refs, samples=samples, slots=sl...  0.83 us
  transfers between devices with their start and end apart: 6, of which 2 were waited for; matrix products, arithmetic and copies ran while one was open for 0% of the time, Pallas kernels for 34%

commit v1 on v0

--- a/solution.py
+++ b/solution.py
@@ -14,7 +14,7 @@
 LOG2E = math.log2(math.e)
 FAR = 4096.0
 CH = 32
-UNROLL = 24
+UNROLL = 32
 LANES = 128
 BLOCK = 128
 ROOM = 24 * 2**20
@@ -336,10 +336,12 @@
         betas[column + 3 * halo] = spread_kappa(right_ref.at[column], tall, samples, segments)
         return carry
 
-    def bring_pair(pair, carry):
-        return bring(2 * pair + 1, bring(2 * pair, carry))
-
-    lax.fori_loop(0, halo // 2, bring_pair, 0)
+    def bring_four(four, carry):
+        for k in range(4):
+            bring(4 * four + k, carry)
+        return carry
+
+    lax.fori_loop(0, halo // 4, bring_four, 0)
     source = noise
     for turn in range(PASSES):
         target = (first_y, second_y)[turn % 2]

time: 32 us -> 32.3 us (level)
  Pallas kernels: 16.7 us -> 20.1 us
  waiting for transfers between devices: 6.79 us -> 3.46 us
    pallas_call x1, Pallas kernels: 8.48 us -> 12 us  [local(): pl.pallas_call(lambda *refs: station_kernel(*refs, samples=samples, width...]
    ppermute x6, waiting for transfers between devices: 6.79 us -> 3.46 us  [shift_to(): lax.ppermute(value, axis, [(source, (source + steps) % count) for source...]
  transfers between devices with their start and end apart: 6 -> 6, of which waited for: 2 -> 1; matrix products, arithmetic and copies ran while one was open for 0% -> 0% of each run, Pallas kernels for 34% -> 45%
where the time goes in v1:
time: 32.3 us; the launch traced here: 31.8 us
  Pallas kernels  20.1 us (62%)
  starting transfers between devices  7.46 us (23%)
  waiting for transfers between devices  3.46 us (11%)
  between operations  0.71 us (2%)
    pallas_call x1, Pallas kernels, local(): pl.pallas_call(lambda *refs: station_kernel(*refs, samples=samples, width...  12 us
    ppermute x6, starting transfers between devices, shift_to(): lax.ppermute(value, axis, [(source, (source + steps) % count) for source...  7.46 us
    pallas_call x1, Pallas kernels, local(): pl.pallas_call(lambda *refs: prior_kernel(*refs, samples=samples, width=w...  5.05 us
    ppermute x6, waiting for transfers between devices, shift_to(): lax.ppermute(value, axis, [(source, (source + steps) % count) for source...  3.46 us
    pallas_call x1, Pallas kernels, local(): pl.pallas_call(lambda *refs: turn_kernel(*refs, samples=samples, width=wi...  2.24 us
    pallas_call x1, Pallas kernels, local(): pl.pallas_call(lambda *refs: pack_kernel(*refs, samples=samples, slots=sl...  0.83 us
  transfers between devices with their start and end apart: 6, of which 1 were waited for; matrix products, arithmetic and copies ran while one was open for 0% of the time, Pallas kernels for 45%

profile of v1, /device:TPU:1, one launch (start us, length us, event | category | flops | bytes accessed | tf_op | source)
XLA Modules:
  0.0 31.8 jit_solution(7240548725936036260)
XLA Ops:
  0.7 0.8 %pack.1.refs_2_ = f32[18,512]{1,0:T(8,128)S(1)} custom-call(f32[1,512]{1,0:T(1,128)} %bitcast.2, f32[1,512]{1,0:T(1,128)} %bitcast.3, f32[16,512]{1,0:T(8,128)} %refs_2_.1, s32[1]{0:T(128)S(6)} %copy.7.refs_3_), custom_call_target="tpu_custom_call" | custom-call | tf_op jit(solution)/shard_map/pack/pallas_call | solution.py:413
  1.5 5.2 %collective-permute-start.5 = (f32[18,512]{1,0:T(8,128)S(1)}, f32[18,512]{1,0:T(8,128)S(1)}, u32[]{:S(2)}, u32[]{:S(2)}) collective-permute-start(f32[18,512]{1,0:T(8,128)S(1)} %pack.1.refs_2_), channel_id=1, source_target_pairs={{0,14},{1,15},{2,0},{3,1},{4,2},{5,3},{6,4},{7,5},{8,6},{9,7},{10,... | collective-permute-start | bytes 110600 | tf_op jit(solution)/shard_map/ppermute | solution.py:399
  6.6 1.0 %collective-permute-start.4 = (f32[18,512]{1,0:T(8,128)S(1)}, f32[18,512]{1,0:T(8,128)S(1)}, u32[]{:S(2)}, u32[]{:S(2)}) collective-permute-start(f32[18,512]{1,0:T(8,128)S(1)} %pack.1.refs_2_), channel_id=1, source_target_pairs={{0,15},{1,0},{2,1},{3,2},{4,3},{5,4},{6,5},{7,6},{8,7},{9,8},{10,9... | collective-permute-start | bytes 110600 | tf_op jit(solution)/shard_map/ppermute | solution.py:399
  7.6 0.8 %collective-permute-start.3 = (f32[18,512]{1,0:T(8,128)S(1)}, f32[18,512]{1,0:T(8,128)S(1)}, u32[]{:S(2)}, u32[]{:S(2)}) collective-permute-start(f32[18,512]{1,0:T(8,128)S(1)} %pack.1.refs_2_), channel_id=1, source_target_pairs={{0,1},{1,2},{2,3},{3,4},{4,5},{5,6},{6,7},{7,8},{8,9},{9,10},{10,1... | collective-permute-start | bytes 110600 | tf_op jit(solution)/shard_map/ppermute | solution.py:399
  8.4 0.0 collective-permute-start.2
  8.4 2.2 %turn.1 = (f32[8,136,128]{2,1,0:T(8,128)S(1)}, f32[8,136,128]{2,1,0:T(8,128)S(1)}, f32[16,128,128]{2,1,0:T(8,128)S(1)}) custom-call(f32[16,16,1024]{2,1,0:T(8,128)} %refs_0_, f32[16,1024]{1,0:T(8,128)} %refs_1_), custom_call_target="tpu_custom_call" | custom-call | tf_op jit(solution)/shard_map/turn/pallas_call | solution.py:431
  10.6 0.1 collective-permute-start
  10.7 0.0 collective-permute-done.5.refs_4_
  10.7 0.5 %collective-permute-start.1 = (f32[8,136,128]{2,1,0:T(8,128)S(1)}, f32[8,136,128]{2,1,0:T(8,128)S(1)}, u32[]{:S(2)}, u32[]{:S(2)}) collective-permute-start(f32[8,136,128]{2,1,0:T(8,128)S(1)} %get-tuple-element.14.refs_1_), channel_id=1, source_target_pairs={{0,15},{1,0},{2,1},{3,2},{4,3},{5,4},{6,5},{7,6},{8,7},{9,8},{10,9... | collective-permute-start | bytes 1671176 | tf_op jit(solution)/shard_map/ppermute | solution.py:399
  11.2 0.0 collective-permute-done.4.refs_3_
  11.2 0.0 collective-permute-done.3.refs_1_
  11.2 3.4 %collective-permute-done.2.refs_0_ = f32[18,512]{1,0:T(8,128)S(1)} collective-permute-done((f32[18,512]{1,0:T(8,128)S(1)}, f32[18,512]{1,0:T(8,128)S(1)}, u32[]{:S(2)}, u32[]{:S(2)}) %collective-permute-start.2) | collective-permute-done | bytes 36896 | tf_op jit(solution)/shard_map/ppermute | solution.py:399
  14.7 12.0 %stations.1.refs_5_ = f32[16,16,1024]{2,1,0:T(8,128)S(1)} custom-call(f32[18,512]{1,0:T(8,128)S(1)} %collective-permute-done.2.refs_0_, f32[18,512]{1,0:T(8,128)S(1)} %collective-permute-done.3.refs_1_, f32[18,512]{1,0:T(8,128)S(1)} %pack.1.refs_2_, f32[18,512]{1,0:T(8,128)S(1)} %collective-permute-done.4.refs_3_, f32[18,512]{1,0:T(8,128)S(1)} %collective-permute-done.5.refs_4_), custom_call_target="tpu_custom_call" | custom-call | flops 10000000000 | bytes 2000000 | tf_op jit(solution)/shard_map/stations/pallas_call | solution.py:454
  26.7 0.0 collective-permute-done.refs_0_
  26.7 0.0 collective-permute-done.1.refs_3_
  26.7 5.0 %prior.1 = f32[16,16,1024]{2,1,0:T(8,128)} custom-call(f32[8,136,128]{2,1,0:T(8,128)S(1)} %collective-permute-done.refs_0_, f32[8,136,128]{2,1,0:T(8,128)S(1)} %get-tuple-element.14.refs_1_, f32[8,136,128]{2,1,0:T(8,128)S(1)} %get-tuple-element.13.refs_2_, f32[8,136,128]{2,1,0:T(8,128)S(1)} %collective-permute-done.1.refs_3_, ...), custom_call_target="tpu_custom_call" | custom-call | tf_op jit(solution)/shard_map/prior/pallas_call | solution.py:480
Async XLA Ops:
  1.5 9.2 %collective-permute-start.5 = (f32[18,512]{1,0:T(8,128)S(1)}, f32[18,512]{1,0:T(8,128)S(1)}, u32[]{:S(2)}, u32[]{:S(2)}) collective-permute-start(f32[18,512]{1,0:T(8,128)S(1)} %pack.1.refs_2_), channel_id=1, source_target_pairs={{0,14},{1,15},{2,0},{3,1},{4,2},{5,3},{6,4},{7,5},{8,6},{9,7},{10,... | collective-permute-start | bytes 110600 | tf_op jit(solution)/shard_map/ppermute | solution.py:399
  6.6 4.6 %collective-permute-start.4 = (f32[18,512]{1,0:T(8,128)S(1)}, f32[18,512]{1,0:T(8,128)S(1)}, u32[]{:S(2)}, u32[]{:S(2)}) collective-permute-start(f32[18,512]{1,0:T(8,128)S(1)} %pack.1.refs_2_), channel_id=1, source_target_pairs={{0,15},{1,0},{2,1},{3,2},{4,3},{5,4},{6,5},{7,6},{8,7},{9,8},{10,9... | collective-permute-start | bytes 110600 | tf_op jit(solution)/shard_map/ppermute | solution.py:399
  7.6 3.6 %collective-permute-start.3 = (f32[18,512]{1,0:T(8,128)S(1)}, f32[18,512]{1,0:T(8,128)S(1)}, u32[]{:S(2)}, u32[]{:S(2)}) collective-permute-start(f32[18,512]{1,0:T(8,128)S(1)} %pack.1.refs_2_), channel_id=1, source_target_pairs={{0,1},{1,2},{2,3},{3,4},{4,5},{5,6},{6,7},{7,8},{8,9},{9,10},{10,1... | collective-permute-start | bytes 110600 | tf_op jit(solution)/shard_map/ppermute | solution.py:399
  8.4 6.3 %collective-permute-start.2 = (f32[18,512]{1,0:T(8,128)S(1)}, f32[18,512]{1,0:T(8,128)S(1)}, u32[]{:S(2)}, u32[]{:S(2)}) collective-permute-start(f32[18,512]{1,0:T(8,128)S(1)} %pack.1.refs_2_), channel_id=1, source_target_pairs={{0,2},{1,3},{2,4},{3,5},{4,6},{5,7},{6,8},{7,9},{8,10},{9,11},{10,... | collective-permute-start | bytes 110600 | tf_op jit(solution)/shard_map/ppermute | solution.py:399
  10.6 16.0 %collective-permute-start = (f32[8,136,128]{2,1,0:T(8,128)S(1)}, f32[8,136,128]{2,1,0:T(8,128)S(1)}, u32[]{:S(2)}, u32[]{:S(2)}) collective-permute-start(f32[8,136,128]{2,1,0:T(8,128)S(1)} %get-tuple-element.13.refs_2_), channel_id=1, source_target_pairs={{0,1},{1,2},{2,3},{3,4},{4,5},{5,6},{6,7},{7,8},{8,9},{9,10},{10,1... | collective-permute-start | bytes 1671176 | tf_op jit(solution)/shard_map/ppermute | solution.py:399
  10.7 16.0 %collective-permute-start.1 = (f32[8,136,128]{2,1,0:T(8,128)S(1)}, f32[8,136,128]{2,1,0:T(8,128)S(1)}, u32[]{:S(2)}, u32[]{:S(2)}) collective-permute-start(f32[8,136,128]{2,1,0:T(8,128)S(1)} %get-tuple-element.14.refs_1_), channel_id=1, source_target_pairs={{0,15},{1,0},{2,1},{3,2},{4,3},{5,4},{6,5},{7,6},{8,7},{9,8},{10,9... | collective-permute-start | bytes 1671176 | tf_op jit(solution)/shard_map/ppermute | solution.py:399

commit v2 on v1

--- a/solution.py
+++ b/solution.py
@@ -14,7 +14,7 @@
 LOG2E = math.log2(math.e)
 FAR = 4096.0
 CH = 32
-UNROLL = 32
+UNROLL = 24
 LANES = 128
 BLOCK = 128
 ROOM = 24 * 2**20

time: 32.3 us -> 31.8 us (0.985)
  Pallas kernels: 20.1 us -> 18.4 us
  waiting for transfers between devices: 3.46 us -> 5.02 us
    pallas_call x1, Pallas kernels: 12 us -> 10.2 us  [local(): pl.pallas_call(lambda *refs: station_kernel(*refs, samples=samples, width...]
    ppermute x6, waiting for transfers between devices: 3.46 us -> 5.02 us  [shift_to(): lax.ppermute(value, axis, [(source, (source + steps) % count) for source...]
  transfers between devices with their start and end apart: 6 -> 6, of which waited for: 1 -> 2; matrix products, arithmetic and copies ran while one was open for 0% -> 0% of each run, Pallas kernels for 45% -> 40%
where the time goes in v2:
time: 31.8 us; the launch traced here: 31.5 us
  Pallas kernels  18.4 us (58%)
  starting transfers between devices  7.46 us (23%)
  waiting for transfers between devices  5.02 us (16%)
  between operations  0.7 us (2%)
    pallas_call x1, Pallas kernels, local(): pl.pallas_call(lambda *refs: station_kernel(*refs, samples=samples, width...  10.2 us
    ppermute x6, starting transfers between devices, shift_to(): lax.ppermute(value, axis, [(source, (source + steps) % count) for source...  7.46 us
    pallas_call x1, Pallas kernels, local(): pl.pallas_call(lambda *refs: prior_kernel(*refs, samples=samples, width=w...  5.05 us
    ppermute x6, waiting for transfers between devices, shift_to(): lax.ppermute(value, axis, [(source, (source + steps) % count) for source...  5.02 us
    pallas_call x1, Pallas kernels, local(): pl.pallas_call(lambda *refs: turn_kernel(*refs, samples=samples, width=wi...  2.24 us
    pallas_call x1, Pallas kernels, local(): pl.pallas_call(lambda *refs: pack_kernel(*refs, samples=samples, slots=sl...  0.83 us
  transfers between devices with their start and end apart: 6, of which 2 were waited for; matrix products, arithmetic and copies ran while one was open for 0% of the time, Pallas kernels for 40%

profile of v2, /device:TPU:1, one launch (start us, length us, event | category | flops | bytes accessed | tf_op | source)
XLA Modules:
  0.0 31.5 jit_solution(16732840596129112)
XLA Ops:
  0.7 0.8 %pack.1.refs_2_ = f32[18,512]{1,0:T(8,128)S(1)} custom-call(f32[1,512]{1,0:T(1,128)} %bitcast.2, f32[1,512]{1,0:T(1,128)} %bitcast.3, f32[16,512]{1,0:T(8,128)} %refs_2_.1, s32[1]{0:T(128)S(6)} %copy.7.refs_3_), custom_call_target="tpu_custom_call" | custom-call | tf_op jit(solution)/shard_map/pack/pallas_call | solution.py:413
  1.5 5.2 %collective-permute-start.5 = (f32[18,512]{1,0:T(8,128)S(1)}, f32[18,512]{1,0:T(8,128)S(1)}, u32[]{:S(2)}, u32[]{:S(2)}) collective-permute-start(f32[18,512]{1,0:T(8,128)S(1)} %pack.1.refs_2_), channel_id=1, source_target_pairs={{0,14},{1,15},{2,0},{3,1},{4,2},{5,3},{6,4},{7,5},{8,6},{9,7},{10,... | collective-permute-start | bytes 110600 | tf_op jit(solution)/shard_map/ppermute | solution.py:399
  6.6 1.0 %collective-permute-start.4 = (f32[18,512]{1,0:T(8,128)S(1)}, f32[18,512]{1,0:T(8,128)S(1)}, u32[]{:S(2)}, u32[]{:S(2)}) collective-permute-start(f32[18,512]{1,0:T(8,128)S(1)} %pack.1.refs_2_), channel_id=1, source_target_pairs={{0,15},{1,0},{2,1},{3,2},{4,3},{5,4},{6,5},{7,6},{8,7},{9,8},{10,9... | collective-permute-start | bytes 110600 | tf_op jit(solution)/shard_map/ppermute | solution.py:399
  7.6 0.8 %collective-permute-start.3 = (f32[18,512]{1,0:T(8,128)S(1)}, f32[18,512]{1,0:T(8,128)S(1)}, u32[]{:S(2)}, u32[]{:S(2)}) collective-permute-start(f32[18,512]{1,0:T(8,128)S(1)} %pack.1.refs_2_), channel_id=1, source_target_pairs={{0,1},{1,2},{2,3},{3,4},{4,5},{5,6},{6,7},{7,8},{8,9},{9,10},{10,1... | collective-permute-start | bytes 110600 | tf_op jit(solution)/shard_map/ppermute | solution.py:399
  8.4 0.0 collective-permute-start.2
  8.4 2.2 %turn.1 = (f32[8,136,128]{2,1,0:T(8,128)S(1)}, f32[8,136,128]{2,1,0:T(8,128)S(1)}, f32[16,128,128]{2,1,0:T(8,128)S(1)}) custom-call(f32[16,16,1024]{2,1,0:T(8,128)} %refs_0_, f32[16,1024]{1,0:T(8,128)} %refs_1_), custom_call_target="tpu_custom_call" | custom-call | tf_op jit(solution)/shard_map/turn/pallas_call | solution.py:431
  10.6 0.1 collective-permute-start
  10.7 0.0 collective-permute-done.5.refs_4_
  10.7 0.5 %collective-permute-start.1 = (f32[8,136,128]{2,1,0:T(8,128)S(1)}, f32[8,136,128]{2,1,0:T(8,128)S(1)}, u32[]{:S(2)}, u32[]{:S(2)}) collective-permute-start(f32[8,136,128]{2,1,0:T(8,128)S(1)} %get-tuple-element.14.refs_1_), channel_id=1, source_target_pairs={{0,15},{1,0},{2,1},{3,2},{4,3},{5,4},{6,5},{7,6},{8,7},{9,8},{10,9... | collective-permute-start | bytes 1671176 | tf_op jit(solution)/shard_map/ppermute | solution.py:399
  11.2 0.0 collective-permute-done.4.refs_3_
  11.2 0.0 collective-permute-done.3.refs_1_
  11.2 3.4 %collective-permute-done.2.refs_0_ = f32[18,512]{1,0:T(8,128)S(1)} collective-permute-done((f32[18,512]{1,0:T(8,128)S(1)}, f32[18,512]{1,0:T(8,128)S(1)}, u32[]{:S(2)}, u32[]{:S(2)}) %collective-permute-start.2) | collective-permute-done | bytes 36896 | tf_op jit(solution)/shard_map/ppermute | solution.py:399
  14.7 10.2 %stations.1.refs_5_ = f32[16,16,1024]{2,1,0:T(8,128)S(1)} custom-call(f32[18,512]{1,0:T(8,128)S(1)} %collective-permute-done.2.refs_0_, f32[18,512]{1,0:T(8,128)S(1)} %collective-permute-done.3.refs_1_, f32[18,512]{1,0:T(8,128)S(1)} %pack.1.refs_2_, f32[18,512]{1,0:T(8,128)S(1)} %collective-permute-done.4.refs_3_, f32[18,512]{1,0:T(8,128)S(1)} %collective-permute-done.5.refs_4_), custom_call_target="tpu_custom_call" | custom-call | flops 10000000000 | bytes 2000000 | tf_op jit(solution)/shard_map/stations/pallas_call | solution.py:454
  24.9 0.0 collective-permute-done.refs_0_
  24.9 1.6 %collective-permute-done.1.refs_3_ = f32[8,136,128]{2,1,0:T(8,128)S(1)} collective-permute-done((f32[8,136,128]{2,1,0:T(8,128)S(1)}, f32[8,136,128]{2,1,0:T(8,128)S(1)}, u32[]{:S(2)}, u32[]{:S(2)}) %collective-permute-start.1) | collective-permute-done | bytes 557088 | tf_op jit(solution)/shard_map/ppermute | solution.py:399
  26.5 5.0 %prior.1 = f32[16,16,1024]{2,1,0:T(8,128)} custom-call(f32[8,136,128]{2,1,0:T(8,128)S(1)} %collective-permute-done.refs_0_, f32[8,136,128]{2,1,0:T(8,128)S(1)} %get-tuple-element.14.refs_1_, f32[8,136,128]{2,1,0:T(8,128)S(1)} %get-tuple-element.13.refs_2_, f32[8,136,128]{2,1,0:T(8,128)S(1)} %collective-permute-done.1.refs_3_, ...), custom_call_target="tpu_custom_call" | custom-call | tf_op jit(solution)/shard_map/prior/pallas_call | solution.py:480
Async XLA Ops:
  1.5 9.2 %collective-permute-start.5 = (f32[18,512]{1,0:T(8,128)S(1)}, f32[18,512]{1,0:T(8,128)S(1)}, u32[]{:S(2)}, u32[]{:S(2)}) collective-permute-start(f32[18,512]{1,0:T(8,128)S(1)} %pack.1.refs_2_), channel_id=1, source_target_pairs={{0,14},{1,15},{2,0},{3,1},{4,2},{5,3},{6,4},{7,5},{8,6},{9,7},{10,... | collective-permute-start | bytes 110600 | tf_op jit(solution)/shard_map/ppermute | solution.py:399
  6.6 4.6 %collective-permute-start.4 = (f32[18,512]{1,0:T(8,128)S(1)}, f32[18,512]{1,0:T(8,128)S(1)}, u32[]{:S(2)}, u32[]{:S(2)}) collective-permute-start(f32[18,512]{1,0:T(8,128)S(1)} %pack.1.refs_2_), channel_id=1, source_target_pairs={{0,15},{1,0},{2,1},{3,2},{4,3},{5,4},{6,5},{7,6},{8,7},{9,8},{10,9... | collective-permute-start | bytes 110600 | tf_op jit(solution)/shard_map/ppermute | solution.py:399
  7.6 3.6 %collective-permute-start.3 = (f32[18,512]{1,0:T(8,128)S(1)}, f32[18,512]{1,0:T(8,128)S(1)}, u32[]{:S(2)}, u32[]{:S(2)}) collective-permute-start(f32[18,512]{1,0:T(8,128)S(1)} %pack.1.refs_2_), channel_id=1, source_target_pairs={{0,1},{1,2},{2,3},{3,4},{4,5},{5,6},{6,7},{7,8},{8,9},{9,10},{10,1... | collective-permute-start | bytes 110600 | tf_op jit(solution)/shard_map/ppermute | solution.py:399
  8.4 6.3 %collective-permute-start.2 = (f32[18,512]{1,0:T(8,128)S(1)}, f32[18,512]{1,0:T(8,128)S(1)}, u32[]{:S(2)}, u32[]{:S(2)}) collective-permute-start(f32[18,512]{1,0:T(8,128)S(1)} %pack.1.refs_2_), channel_id=1, source_target_pairs={{0,2},{1,3},{2,4},{3,5},{4,6},{5,7},{6,8},{7,9},{8,10},{9,11},{10,... | collective-permute-start | bytes 110600 | tf_op jit(solution)/shard_map/ppermute | solution.py:399
  10.6 14.3 %collective-permute-start = (f32[8,136,128]{2,1,0:T(8,128)S(1)}, f32[8,136,128]{2,1,0:T(8,128)S(1)}, u32[]{:S(2)}, u32[]{:S(2)}) collective-permute-start(f32[8,136,128]{2,1,0:T(8,128)S(1)} %get-tuple-element.13.refs_2_), channel_id=1, source_target_pairs={{0,1},{1,2},{2,3},{3,4},{4,5},{5,6},{6,7},{7,8},{8,9},{9,10},{10,1... | collective-permute-start | bytes 1671176 | tf_op jit(solution)/shard_map/ppermute | solution.py:399
  10.7 15.8 %collective-permute-start.1 = (f32[8,136,128]{2,1,0:T(8,128)S(1)}, f32[8,136,128]{2,1,0:T(8,128)S(1)}, u32[]{:S(2)}, u32[]{:S(2)}) collective-permute-start(f32[8,136,128]{2,1,0:T(8,128)S(1)} %get-tuple-element.14.refs_1_), channel_id=1, source_target_pairs={{0,15},{1,0},{2,1},{3,2},{4,3},{5,4},{6,5},{7,6},{8,7},{9,8},{10,9... | collective-permute-start | bytes 1671176 | tf_op jit(solution)/shard_map/ppermute | solution.py:399
